TPU v7x, 32 devices: a whole 2x2x4 slice. The times are simulated.
32 devices in a mesh: dom: 16 (over z, y, core), orb: 2 (over x).
Axes of the slice: x: 2, y: 2, z: 4, core: 2. Of those that a mesh axis runs over, the one named last changes fastest.
Arguments:
- orbitals: float32 [6144, 1024], P('dom', 'orb'), may hold values from -6 to 6
- cell_mats: float32 [16, 512, 512], P('dom'), as said below
- cell_map: int32 [16, 512], P('dom'), may hold values from 0 to 511, as said below
Outputs:
- rotated: float32 [6144, 1024], P(('dom', 'orb'))
Inputs may be any that keep to these rules, and one draw needn't show every extreme that they name: `cell_map`: cell c belongs to domain c. Its 512 entries are distinct. Entries below 384 name the domain's own nodes, each used by some cell of the domain; an entry j >= 384 names own node j - 384 of the next domain, and every such j is used by some cell of the domain. `cell_mats`: each cell matrix is symmetric.
All inputs are finite; a program needn't handle non-finite values.
Results may differ from a plain program's by a relative error of at most 0.00013.
Values sent between devices are 32-bit elements; how exact they have to be, the bound alone decides.
No kernel may reach another device: no remote copies, remote signals or barrier semaphores. Data moves between devices by JAX's collectives and lax.ppermute only.
A program may use at most 64 MiB of HBM per device.

v0:
```python
import jax
import jax.numpy as jnp
from jax import lax
from jax.sharding import PartitionSpec as P

DEGREE = 5
HALO = 128
filter_center = 2.0
filter_half = 3.5


def shifted(block, axis, distance):
    devices = range(lax.axis_size(axis))
    route = [((i - distance) % len(devices), i) for i in devices]
    return lax.ppermute(block, axis, route)


def apply_local(vectors, cell_mats, cell_map):
    own_count = vectors.shape[0]
    borrowed = shifted(vectors[:HALO], "dom", -1)
    extended = jnp.concatenate([vectors, borrowed], axis=0)
    summed = jnp.zeros(extended.shape, jnp.float32)
    node_idx = cell_map[0]
    gathered = jnp.take(extended, node_idx, axis=0)
    product = jnp.dot(
        cell_mats[0], gathered, precision=lax.Precision.HIGHEST, preferred_element_type=jnp.float32
    )
    summed = summed.at[node_idx].add(product)
    returned = shifted(summed[own_count:], "dom", 1)
    return jnp.concatenate([summed[:HALO] + returned, summed[HALO:own_count]], axis=0)


def body(orbitals, cell_mats, cell_map):
    own_count = orbitals.shape[0]
    node_total = own_count * lax.axis_size("dom")
    previous = orbitals
    current = (apply_local(orbitals, cell_mats, cell_map) - filter_center * orbitals) / filter_half
    for order in range(1, DEGREE):
        advanced = (
            2.0
            * (apply_local(current, cell_mats, cell_map) - filter_center * current)
            / filter_half
            - previous
        )
        previous, current = (current, advanced)
    regrouped = lax.all_to_all(current, "orb", split_axis=0, concat_axis=1, tiled=True)
    local_gram = jnp.einsum("nk,nj->kj", regrouped, regrouped, precision=lax.Precision.HIGHEST)
    gram = lax.psum(local_gram, ("dom", "orb"))
    gram = gram / node_total
    lower = jnp.linalg.cholesky(gram)
    solved = lax.linalg.triangular_solve(lower, regrouped.T, left_side=True, lower=True)
    return solved.T


def solution(mesh):
    placed = (P("dom", "orb"), P("dom", None, None), P("dom", None))
    return jax.shard_map(
        body, mesh=mesh, in_specs=placed, out_specs=P(("dom", "orb"), None), check_vma=False
    )
```

profile of v0, /device:TPU:0, one launch (start us, length us, event | category | flops | bytes accessed | tf_op | source)
XLA Modules:
  0.0 657.8 jit_solution(3789338286109253911)
XLA Ops:
  7.6 5.5 collective-permute-start
  20.6 4.9 convolution_bitcast_fusion.4
  26.8 4.5 scatter_custom_fusion
  31.4 8.7 %collective-permute-done.1 = f32[128,512]{1,0:T(8,128)S(1)} collective-permute-done((f32[128,512]{1,0:T(8,128)S(1)}, f32[128,512]{1,0:T(8,128)S(1)}, u32[]{:S(2)}, u32[]{:S(2)}) %collective-permute-start.1) | collective-permute-done | bytes 262176 | tf_op jit(solution)/shard_map/ppermute | solution.py:15
  40.9 3.8 collective-permute-done.2
  47.1 4.8 convolution_bitcast_fusion.3
  53.2 4.5 scatter_custom_fusion.1
  57.8 8.7 %collective-permute-done.3 = f32[128,512]{1,0:T(8,128)S(1)} collective-permute-done((f32[128,512]{1,0:T(8,128)S(1)}, f32[128,512]{1,0:T(8,128)S(1)}, u32[]{:S(2)}, u32[]{:S(2)}) %collective-permute-start.3) | collective-permute-done | bytes 262176 | tf_op jit(solution)/shard_map/ppermute | solution.py:15
  68.4 3.9 collective-permute-done.4
  74.0 4.6 convolution_bitcast_fusion.2
  78.6 2.6 copy.21
  81.2 4.5 scatter_custom_fusion.2
  85.8 8.7 %collective-permute-done.5 = f32[128,512]{1,0:T(8,128)S(1)} collective-permute-done((f32[128,512]{1,0:T(8,128)S(1)}, f32[128,512]{1,0:T(8,128)S(1)}, u32[]{:S(2)}, u32[]{:S(2)}) %collective-permute-start.5) | collective-permute-done | bytes 262176 | tf_op jit(solution)/shard_map/ppermute | solution.py:15
  96.3 3.9 collective-permute-done.6
  102.6 5.8 convolution_bitcast_fusion.1
  108.4 2.6 copy.22
  111.0 5.3 scatter_custom_fusion.3
  118.4 7.7 %collective-permute-done.7 = f32[128,512]{1,0:T(8,128)S(1)} collective-permute-done((f32[128,512]{1,0:T(8,128)S(1)}, f32[128,512]{1,0:T(8,128)S(1)}, u32[]{:S(2)}, u32[]{:S(2)}) %collective-permute-start.7) | collective-permute-done | bytes 262176 | tf_op jit(solution)/shard_map/ppermute | solution.py:15
  127.6 3.9 collective-permute-done.8
  134.0 5.8 convolution_bitcast_fusion
  139.8 2.6 copy.23
  142.4 4.5 scatter_custom_fusion.4
  147.0 8.6 %collective-permute-done.9 = f32[128,512]{1,0:T(8,128)S(1)} collective-permute-done((f32[128,512]{1,0:T(8,128)S(1)}, f32[128,512]{1,0:T(8,128)S(1)}, u32[]{:S(2)}, u32[]{:S(2)}) %collective-permute-start.9) | collective-permute-done | bytes 262176 | tf_op jit(solution)/shard_map/ppermute | solution.py:15
  156.0 10.5 %all_to_all.19 = f32[2,192,512]{2,1,0:T(8,128)S(1)} all-to-all(f32[2,192,512]{2,1,0:T(8,128)S(1)} %bitcast.145), channel_id=1, replica_groups=mesh['dom'=16,'orb'=2] {'orb'}, dimensions={0} | all-to-all | bytes 1572864 | tf_op jit(solution)/shard_map/all_to_all | solution.py:46
  166.6 5.1 fusion.106
  171.7 139.4 %all-reduce.3.cloned.1.call-done = f32[1024,1024]{0,1:T(8,128)} async-done(((f32[1024,1024]{0,1:T(8,128)}), f32[1024,1024]{0,1:T(8,128)}) %all-reduce.3.cloned.1.call-update) | async-done | bytes 4194320 | tf_op jit(solution)/shard_map/psum | solution.py:48
  311.1 5.1 broadcast_multiply_fusion
  316.2 5.7 copy.26
  321.9 4.5 fusion
  328.3 11.7 %cholesky.223 = f32[128,128]{1,0:T(8,128)S(1)} custom-call(f32[128,128]{1,0:T(8,128)S(1)} %cholesky.580), custom_call_target="Cholesky" | custom-call | tf_op jit(solution)/shard_map/jit(cholesky)/cholesky | solution.py:50
  340.0 2.5 cholesky.255
  342.5 9.8 %custom-call.62 = f32[1,128,128]{1,2,0:T(8,128)S(1)} custom-call(f32[1,128,128]{2,1,0:T(8,128)S(1)} %get-tuple-element.70), custom_call_target="InvertDiagBlocksLowerTriangular" | custom-call | tf_op jit(solution)/shard_map/jit(cholesky)/cholesky | solution.py:50
  356.3 11.8 %cholesky.244 = f32[128,128]{1,0:T(8,128)S(1)} custom-call(f32[128,128]{1,0:T(8,128)S(1)} %cholesky.584), custom_call_target="Cholesky" | custom-call | tf_op jit(solution)/shard_map/jit(cholesky)/cholesky | solution.py:50
  368.8 9.8 %custom-call.63 = f32[1,128,128]{1,2,0:T(8,128)S(1)} custom-call(f32[1,128,128]{2,1,0:T(8,128)S(1)} %get-tuple-element.67), custom_call_target="InvertDiagBlocksLowerTriangular" | custom-call | tf_op jit(solution)/shard_map/jit(cholesky)/cholesky | solution.py:50
  382.0 11.7 %cholesky.468 = f32[128,128]{1,0:T(8,128)S(1)} custom-call(f32[128,128]{1,0:T(8,128)S(1)} %cholesky.589), custom_call_target="Cholesky" | custom-call | tf_op jit(solution)/shard_map/jit(cholesky)/cholesky | solution.py:50
  394.9 9.8 %custom-call.64 = f32[1,128,128]{1,2,0:T(8,128)S(1)} custom-call(f32[1,128,128]{2,1,0:T(8,128)S(1)} %get-tuple-element.64), custom_call_target="InvertDiagBlocksLowerTriangular" | custom-call | tf_op jit(solution)/shard_map/jit(cholesky)/cholesky | solution.py:50
  408.3 11.9 %cholesky.487 = f32[128,128]{1,0:T(8,128)S(1)} custom-call(f32[128,128]{1,0:T(8,128)S(1)} %cholesky.594), custom_call_target="Cholesky" | custom-call | tf_op jit(solution)/shard_map/jit(cholesky)/cholesky | solution.py:50
  421.5 9.8 %custom-call.65 = f32[1,128,128]{1,2,0:T(8,128)S(1)} custom-call(f32[1,128,128]{2,1,0:T(8,128)S(1)} %get-tuple-element.61), custom_call_target="InvertDiagBlocksLowerTriangular" | custom-call | tf_op jit(solution)/shard_map/jit(cholesky)/cholesky | solution.py:50
  434.7 11.7 %cholesky.506 = f32[128,128]{1,0:T(8,128)S(1)} custom-call(f32[128,128]{1,0:T(8,128)S(1)} %cholesky.599), custom_call_target="Cholesky" | custom-call | tf_op jit(solution)/shard_map/jit(cholesky)/cholesky | solution.py:50
  447.7 10.2 %custom-call.66 = f32[1,128,128]{1,2,0:T(8,128)S(1)} custom-call(f32[1,128,128]{2,1,0:T(8,128)S(1)} %get-tuple-element.58), custom_call_target="InvertDiagBlocksLowerTriangular" | custom-call | tf_op jit(solution)/shard_map/jit(cholesky)/cholesky | solution.py:50
  461.3 11.7 %cholesky.526 = f32[128,128]{1,0:T(8,128)S(1)} custom-call(f32[128,128]{1,0:T(8,128)S(1)} %cholesky.604), custom_call_target="Cholesky" | custom-call | tf_op jit(solution)/shard_map/jit(cholesky)/cholesky | solution.py:50
  474.3 9.8 %custom-call.67 = f32[1,128,128]{1,2,0:T(8,128)S(1)} custom-call(f32[1,128,128]{2,1,0:T(8,128)S(1)} %get-tuple-element.55), custom_call_target="InvertDiagBlocksLowerTriangular" | custom-call | tf_op jit(solution)/shard_map/jit(cholesky)/cholesky | solution.py:50
  487.1 11.9 %cholesky.546 = f32[128,128]{1,0:T(8,128)S(1)} custom-call(f32[128,128]{1,0:T(8,128)S(1)} %cholesky.609), custom_call_target="Cholesky" | custom-call | tf_op jit(solution)/shard_map/jit(cholesky)/cholesky | solution.py:50
  500.2 9.8 %custom-call.68 = f32[1,128,128]{1,2,0:T(8,128)S(1)} custom-call(f32[1,128,128]{2,1,0:T(8,128)S(1)} %get-tuple-element.52), custom_call_target="InvertDiagBlocksLowerTriangular" | custom-call | tf_op jit(solution)/shard_map/jit(cholesky)/cholesky | solution.py:50
  512.6 11.7 %cholesky.564 = f32[128,128]{1,0:T(8,128)S(1)} custom-call(f32[128,128]{1,0:T(8,128)S(1)} %convolution_subtract_fusion.13), custom_call_target="Cholesky" | custom-call | tf_op jit(solution)/shard_map/jit(cholesky)/cholesky | solution.py:50
  531.2 4.8 select_select_fusion
  536.0 22.8 %while.1 = (s32[]{:T(128)}, f32[1024,1024]{1,0:T(8,128)}, s32[8,2]{0,1:T(2,128)S(1)}, f32[8,128,128]{2,1,0:T(8,128)S(1)}, s32[]{:T(128)}) while((s32[]{:T(128)}, f32[1024,1024]{1,0:T(8,128)}, s32[8,2]{0,1:T(2,128)S(1)}, f32[8,128,128]{2,1,0:T(8,128)S(1)}, s32[]{:T(128)}) %tuple.58), condition=%wide.while_cond, body=%wide.while_body.sunk | while | flops 2 | bytes 131181 | solution.py:51
  558.8 78.8 %custom-call.69 = f32[8,128,128]{1,2,0:T(8,128)S(1)} custom-call(f32[8,128,128]{2,1,0:T(8,128)S(1)} %get-tuple-element.13), custom_call_target="InvertDiagBlocksLowerTriangular" | custom-call | tf_op jit(solution)/shard_map/triangular_solve | solution.py:51
  (156 shorter events, 98.7 us)
Async XLA Ops:
  6.5 14.0 %copy-start = (f32[1,512,512]{2,1,0:T(8,128)S(1)}, f32[1,512,512]{2,1,0:T(8,128)}, u32[]{:S(2)}) copy-start(f32[1,512,512]{2,1,0:T(8,128)} %param.6) | copy-start | bytes 3145732
  6.5 304.5 %all-reduce.3.cloned.1.call-start = ((), (), s32[]{:S(2)}) async-start(), calls=%async_computation.1 | async-start | bytes 8388608 | tf_op jit(solution)/shard_map/psum | solution.py:48
  7.6 9.4 %collective-permute-start = (f32[128,512]{1,0:T(8,128)S(1)}, f32[128,512]{1,0:T(8,128)S(1)}, u32[]{:S(2)}, u32[]{:S(2)}) collective-permute-start(f32[128,512]{1,0:T(8,128)S(1)} %slice.283), channel_id=1, source_target_pairs={{2,0},{4,2},{6,4},{8,6},{10,8},{12,10},{14,12},{16,14},{18,16},{20... | collective-permute-start | bytes 786440 | tf_op jit(solution)/shard_map/ppermute | solution.py:15
  20.6 19.6 %copy-start.6 = (f32[384,512]{1,0:T(8,128)S(1)}, f32[384,512]{1,0:T(8,128)}, u32[]{:S(2)}) copy-start(f32[384,512]{1,0:T(8,128)} %param.5) | copy-start | bytes 2359300
  31.3 8.8 %collective-permute-start.1 = (f32[128,512]{1,0:T(8,128)S(1)}, f32[128,512]{1,0:T(8,128)S(1)}, u32[]{:S(2)}, u32[]{:S(2)}) collective-permute-start(f32[128,512]{1,0:T(8,128)S(1)} %slice.325), channel_id=1, source_target_pairs={{30,0},{0,2},{2,4},{4,6},{6,8},{8,10},{10,12},{12,14},{14,16},{16,... | collective-permute-start | bytes 786440 | tf_op jit(solution)/shard_map/ppermute | solution.py:15
  40.2 0.7 copy-start.10
  40.4 4.3 copy-start.7
  40.4 4.2 collective-permute-start.2
  57.7 8.8 %collective-permute-start.3 = (f32[128,512]{1,0:T(8,128)S(1)}, f32[128,512]{1,0:T(8,128)S(1)}, u32[]{:S(2)}, u32[]{:S(2)}) collective-permute-start(f32[128,512]{1,0:T(8,128)S(1)} %slice.329), channel_id=1, source_target_pairs={{30,0},{0,2},{2,4},{4,6},{6,8},{8,10},{10,12},{12,14},{14,16},{16,... | collective-permute-start | bytes 786440 | tf_op jit(solution)/shard_map/ppermute | solution.py:15
  67.8 4.5 copy-start.2
  67.8 4.5 collective-permute-start.4
  74.0 20.6 %copy-start.3 = (f32[384,512]{1,0:T(8,128)S(1)}, f32[384,512]{1,0:T(8,128)}, u32[]{:S(2)}) copy-start(f32[384,512]{1,0:T(8,128)} %copy-done.2) | copy-start | bytes 2359300
  85.7 8.8 %collective-permute-start.5 = (f32[128,512]{1,0:T(8,128)S(1)}, f32[128,512]{1,0:T(8,128)S(1)}, u32[]{:S(2)}, u32[]{:S(2)}) collective-permute-start(f32[128,512]{1,0:T(8,128)S(1)} %slice.333), channel_id=1, source_target_pairs={{30,0},{0,2},{2,4},{4,6},{6,8},{8,10},{10,12},{12,14},{14,16},{16,... | collective-permute-start | bytes 786440 | tf_op jit(solution)/shard_map/ppermute | solution.py:15
  96.0 4.1 collective-permute-start.6
  102.6 24.5 %copy-start.4 = (f32[384,512]{1,0:T(8,128)S(1)}, f32[384,512]{1,0:T(8,128)}, u32[]{:S(2)}) copy-start(f32[384,512]{1,0:T(8,128)} %copy-done.2) | copy-start | bytes 2359300
  117.2 8.8 %collective-permute-start.7 = (f32[128,512]{1,0:T(8,128)S(1)}, f32[128,512]{1,0:T(8,128)S(1)}, u32[]{:S(2)}, u32[]{:S(2)}) collective-permute-start(f32[128,512]{1,0:T(8,128)S(1)} %slice.337), channel_id=1, source_target_pairs={{30,0},{0,2},{2,4},{4,6},{6,8},{8,10},{10,12},{12,14},{14,16},{16,... | collective-permute-start | bytes 786440 | tf_op jit(solution)/shard_map/ppermute | solution.py:15
  127.3 4.2 copy-start.8
  127.4 4.2 collective-permute-start.8
  134.0 21.7 %copy-start.9 = (f32[384,512]{1,0:T(8,128)S(1)}, f32[384,512]{1,0:T(8,128)}, u32[]{:S(2)}) copy-start(f32[384,512]{1,0:T(8,128)} %copy-done.8) | copy-start | bytes 2359300
  146.9 8.7 %collective-permute-start.9 = (f32[128,512]{1,0:T(8,128)S(1)}, f32[128,512]{1,0:T(8,128)S(1)}, u32[]{:S(2)}, u32[]{:S(2)}) collective-permute-start(f32[128,512]{1,0:T(8,128)S(1)} %slice.341), channel_id=1, source_target_pairs={{30,0},{0,2},{2,4},{4,6},{6,8},{8,10},{10,12},{12,14},{14,16},{16,... | collective-permute-start | bytes 786440 | tf_op jit(solution)/shard_map/ppermute | solution.py:15
  326.4 1.9 copy-start.5
  639.2 11.5 %copy-start.1 = (f32[1,512,512]{2,1,0:T(8,128)S(1)}, f32[1,512,512]{2,1,0:T(8,128)}, u32[]{:S(2)}) copy-start(f32[1,512,512]{2,1,0:T(8,128)} %param.6) | copy-start | bytes 3145732
  649.8 0.9 copy-start.11
Sparse Core Ops, SparseCore 0:
  171.8 139.2 all-reduce.2
where the time goes:
time: 666 us; the launch traced here: 658 us
  other arithmetic  297 us (45%)
  waiting for transfers between devices  199 us (30%)
  matrix products  66.2 us (10%)
  local copies, waits for them, and re-layouts  58.8 us (9%)
  between operations  19.1 us (3%)
  blocking collectives  10.5 us (2%)
  starting transfers between devices  7.25 us (1%)
    another operation x30, other arithmetic, body(): lower = jnp.linalg.cholesky(gram)  172 us
    psum x1, waiting for transfers between devices, body(): gram = lax.psum(local_gram, ('dom', 'orb'))  139 us
    another operation x3, other arithmetic, body(): lax.linalg.triangular_solve(lower, regrouped.T, left_side=True, lower=True)  83.6 us
    ppermute x10, waiting for transfers between devices, shifted(): return lax.ppermute(block, axis, route)  59.6 us
    dot_general x5, matrix products, apply_local(): jnp.dot(cell_mats[0], gathered, precision=lax.Precision.HIGHEST, preferre...  25.9 us
    scatter-add x5, other arithmetic, apply_local(): summed = summed.at[node_idx].add(product)  23.3 us
    another operation x14, matrix products, body(): lower = jnp.linalg.cholesky(gram)  23.1 us
    another operation x24, local copies, waits for them, and re-layouts  22.7 us
  transfers between devices with their start and end apart: 11, of which 11 were waited for; matrix products, arithmetic and copies ran while one was open for 1% of the time, Pallas kernels for 0%

commit v1 on v0

--- a/solution.py
+++ b/solution.py
@@ -45,7 +45,7 @@
         previous, current = (current, advanced)
     regrouped = lax.all_to_all(current, "orb", split_axis=0, concat_axis=1, tiled=True)
     local_gram = jnp.einsum("nk,nj->kj", regrouped, regrouped, precision=lax.Precision.HIGHEST)
-    gram = lax.psum(local_gram, ("dom", "orb"))
+    gram = lax.psum(lax.psum(local_gram, "orb"), "dom")
     gram = gram / node_total
     lower = jnp.linalg.cholesky(gram)
     solved = lax.linalg.triangular_solve(lower, regrouped.T, left_side=True, lower=True)

time: 666 us -> 746 us (1.12)
  waiting for transfers between devices: 199 us -> 279 us
    psum x1 -> x2, waiting for transfers between devices: 139 us -> 220 us  [body(): gram = lax.psum(lax.psum(local_gram, 'orb'), 'dom')]
  transfers between devices with their start and end apart: 11 -> 12, of which waited for: 11 -> 12; matrix products, arithmetic and copies ran while one was open for 1% -> 0% of each run, Pallas kernels for 0% -> 0%
where the time goes in v1:
time: 746 us; the launch traced here: 738 us
  other arithmetic  297 us (40%)
  waiting for transfers between devices  279 us (37%)
  matrix products  66.1 us (9%)
  local copies, waits for them, and re-layouts  58.8 us (8%)
  between operations  19.2 us (3%)
  blocking collectives  10.5 us (1%)
    psum x2, waiting for transfers between devices, body(): gram = lax.psum(lax.psum(local_gram, 'orb'), 'dom')  220 us
    another operation x30, other arithmetic, body(): lower = jnp.linalg.cholesky(gram)  172 us
    another operation x3, other arithmetic, body(): lax.linalg.triangular_solve(lower, regrouped.T, left_side=True, lower=True)  83.6 us
    ppermute x10, waiting for transfers between devices, shifted(): return lax.ppermute(block, axis, route)  59.6 us
    dot_general x5, matrix products, apply_local(): jnp.dot(cell_mats[0], gathered, precision=lax.Precision.HIGHEST, preferre...  25.9 us
    scatter-add x5, other arithmetic, apply_local(): summed = summed.at[node_idx].add(product)  23.3 us
    another operation x14, matrix products, body(): lower = jnp.linalg.cholesky(gram)  23.1 us
    another operation x24, local copies, waits for them, and re-layouts  22.7 us
  transfers between devices with their start and end apart: 12, of which 12 were waited for; matrix products, arithmetic and copies ran while one was open for 0% of the time, Pallas kernels for 0%

profile of v1, /device:TPU:0, one launch (start us, length us, event | category | flops | bytes accessed | tf_op | source)
XLA Modules:
  0.0 738.1 jit_solution(2441147235073197298)
XLA Ops:
  7.6 5.5 collective-permute-start
  20.6 4.9 convolution_bitcast_fusion.4
  26.8 4.5 scatter_custom_fusion
  31.4 8.7 %collective-permute-done.1 = f32[128,512]{1,0:T(8,128)S(1)} collective-permute-done((f32[128,512]{1,0:T(8,128)S(1)}, f32[128,512]{1,0:T(8,128)S(1)}, u32[]{:S(2)}, u32[]{:S(2)}) %collective-permute-start.1) | collective-permute-done | bytes 262176 | tf_op jit(solution)/shard_map/ppermute | solution.py:15
  40.9 3.8 collective-permute-done.2
  47.1 4.8 convolution_bitcast_fusion.3
  53.2 4.5 scatter_custom_fusion.1
  57.8 8.7 %collective-permute-done.3 = f32[128,512]{1,0:T(8,128)S(1)} collective-permute-done((f32[128,512]{1,0:T(8,128)S(1)}, f32[128,512]{1,0:T(8,128)S(1)}, u32[]{:S(2)}, u32[]{:S(2)}) %collective-permute-start.3) | collective-permute-done | bytes 262176 | tf_op jit(solution)/shard_map/ppermute | solution.py:15
  68.4 3.9 collective-permute-done.4
  74.0 4.6 convolution_bitcast_fusion.2
  78.6 2.6 copy.21
  81.2 4.5 scatter_custom_fusion.2
  85.8 8.7 %collective-permute-done.5 = f32[128,512]{1,0:T(8,128)S(1)} collective-permute-done((f32[128,512]{1,0:T(8,128)S(1)}, f32[128,512]{1,0:T(8,128)S(1)}, u32[]{:S(2)}, u32[]{:S(2)}) %collective-permute-start.5) | collective-permute-done | bytes 262176 | tf_op jit(solution)/shard_map/ppermute | solution.py:15
  96.3 3.9 collective-permute-done.6
  102.6 5.8 convolution_bitcast_fusion.1
  108.4 2.6 copy.22
  111.0 5.3 scatter_custom_fusion.3
  118.4 7.7 %collective-permute-done.7 = f32[128,512]{1,0:T(8,128)S(1)} collective-permute-done((f32[128,512]{1,0:T(8,128)S(1)}, f32[128,512]{1,0:T(8,128)S(1)}, u32[]{:S(2)}, u32[]{:S(2)}) %collective-permute-start.7) | collective-permute-done | bytes 262176 | tf_op jit(solution)/shard_map/ppermute | solution.py:15
  127.6 3.9 collective-permute-done.8
  134.0 5.8 convolution_bitcast_fusion
  139.8 2.6 copy.23
  142.4 4.5 scatter_custom_fusion.4
  147.0 8.6 %collective-permute-done.9 = f32[128,512]{1,0:T(8,128)S(1)} collective-permute-done((f32[128,512]{1,0:T(8,128)S(1)}, f32[128,512]{1,0:T(8,128)S(1)}, u32[]{:S(2)}, u32[]{:S(2)}) %collective-permute-start.9) | collective-permute-done | bytes 262176 | tf_op jit(solution)/shard_map/ppermute | solution.py:15
  156.0 10.5 %all_to_all.19 = f32[2,192,512]{2,1,0:T(8,128)S(1)} all-to-all(f32[2,192,512]{2,1,0:T(8,128)S(1)} %bitcast.145), channel_id=1, replica_groups=mesh['dom'=16,'orb'=2] {'orb'}, dimensions={0} | all-to-all | bytes 1572864 | tf_op jit(solution)/shard_map/all_to_all | solution.py:46
  166.6 5.0 fusion.106
  171.7 105.0 %all-reduce.4.cloned.1.call-done = f32[1024,1024]{0,1:T(8,128)} async-done(((f32[1024,1024]{0,1:T(8,128)}), f32[1024,1024]{0,1:T(8,128)}) %all-reduce.4.cloned.1.call-update) | async-done | bytes 4194320 | tf_op jit(solution)/shard_map/psum | solution.py:48
  276.7 114.7 %all-reduce.6.cloned.1.call-done = f32[1024,1024]{0,1:T(8,128)} async-done(((f32[1024,1024]{0,1:T(8,128)}), f32[1024,1024]{0,1:T(8,128)}) %all-reduce.6.cloned.1.call-update) | async-done | bytes 4194320 | tf_op jit(solution)/shard_map/psum | solution.py:48
  391.4 5.1 broadcast_multiply_fusion
  396.5 5.7 copy.26
  402.2 4.5 fusion
  408.7 11.7 %cholesky.223 = f32[128,128]{1,0:T(8,128)S(1)} custom-call(f32[128,128]{1,0:T(8,128)S(1)} %cholesky.580), custom_call_target="Cholesky" | custom-call | tf_op jit(solution)/shard_map/jit(cholesky)/cholesky | solution.py:50
  422.9 9.8 %custom-call.62 = f32[1,128,128]{1,2,0:T(8,128)S(1)} custom-call(f32[1,128,128]{2,1,0:T(8,128)S(1)} %get-tuple-element.70), custom_call_target="InvertDiagBlocksLowerTriangular" | custom-call | tf_op jit(solution)/shard_map/jit(cholesky)/cholesky | solution.py:50
  436.7 11.8 %cholesky.244 = f32[128,128]{1,0:T(8,128)S(1)} custom-call(f32[128,128]{1,0:T(8,128)S(1)} %cholesky.584), custom_call_target="Cholesky" | custom-call | tf_op jit(solution)/shard_map/jit(cholesky)/cholesky | solution.py:50
  449.1 9.8 %custom-call.63 = f32[1,128,128]{1,2,0:T(8,128)S(1)} custom-call(f32[1,128,128]{2,1,0:T(8,128)S(1)} %get-tuple-element.67), custom_call_target="InvertDiagBlocksLowerTriangular" | custom-call | tf_op jit(solution)/shard_map/jit(cholesky)/cholesky | solution.py:50
  462.3 11.7 %cholesky.468 = f32[128,128]{1,0:T(8,128)S(1)} custom-call(f32[128,128]{1,0:T(8,128)S(1)} %cholesky.589), custom_call_target="Cholesky" | custom-call | tf_op jit(solution)/shard_map/jit(cholesky)/cholesky | solution.py:50
  475.3 9.8 %custom-call.64 = f32[1,128,128]{1,2,0:T(8,128)S(1)} custom-call(f32[1,128,128]{2,1,0:T(8,128)S(1)} %get-tuple-element.64), custom_call_target="InvertDiagBlocksLowerTriangular" | custom-call | tf_op jit(solution)/shard_map/jit(cholesky)/cholesky | solution.py:50
  488.6 11.9 %cholesky.487 = f32[128,128]{1,0:T(8,128)S(1)} custom-call(f32[128,128]{1,0:T(8,128)S(1)} %cholesky.594), custom_call_target="Cholesky" | custom-call | tf_op jit(solution)/shard_map/jit(cholesky)/cholesky | solution.py:50
  501.8 9.8 %custom-call.65 = f32[1,128,128]{1,2,0:T(8,128)S(1)} custom-call(f32[1,128,128]{2,1,0:T(8,128)S(1)} %get-tuple-element.61), custom_call_target="InvertDiagBlocksLowerTriangular" | custom-call | tf_op jit(solution)/shard_map/jit(cholesky)/cholesky | solution.py:50
  515.1 11.7 %cholesky.506 = f32[128,128]{1,0:T(8,128)S(1)} custom-call(f32[128,128]{1,0:T(8,128)S(1)} %cholesky.599), custom_call_target="Cholesky" | custom-call | tf_op jit(solution)/shard_map/jit(cholesky)/cholesky | solution.py:50
  528.1 10.2 %custom-call.66 = f32[1,128,128]{1,2,0:T(8,128)S(1)} custom-call(f32[1,128,128]{2,1,0:T(8,128)S(1)} %get-tuple-element.58), custom_call_target="InvertDiagBlocksLowerTriangular" | custom-call | tf_op jit(solution)/shard_map/jit(cholesky)/cholesky | solution.py:50
  541.6 11.7 %cholesky.526 = f32[128,128]{1,0:T(8,128)S(1)} custom-call(f32[128,128]{1,0:T(8,128)S(1)} %cholesky.604), custom_call_target="Cholesky" | custom-call | tf_op jit(solution)/shard_map/jit(cholesky)/cholesky | solution.py:50
  554.6 9.8 %custom-call.67 = f32[1,128,128]{1,2,0:T(8,128)S(1)} custom-call(f32[1,128,128]{2,1,0:T(8,128)S(1)} %get-tuple-element.55), custom_call_target="InvertDiagBlocksLowerTriangular" | custom-call | tf_op jit(solution)/shard_map/jit(cholesky)/cholesky | solution.py:50
  567.4 11.9 %cholesky.546 = f32[128,128]{1,0:T(8,128)S(1)} custom-call(f32[128,128]{1,0:T(8,128)S(1)} %cholesky.609), custom_call_target="Cholesky" | custom-call | tf_op jit(solution)/shard_map/jit(cholesky)/cholesky | solution.py:50
  580.5 9.8 %custom-call.68 = f32[1,128,128]{1,2,0:T(8,128)S(1)} custom-call(f32[1,128,128]{2,1,0:T(8,128)S(1)} %get-tuple-element.52), custom_call_target="InvertDiagBlocksLowerTriangular" | custom-call | tf_op jit(solution)/shard_map/jit(cholesky)/cholesky | solution.py:50
  593.0 11.7 %cholesky.564 = f32[128,128]{1,0:T(8,128)S(1)} custom-call(f32[128,128]{1,0:T(8,128)S(1)} %convolution_subtract_fusion.13), custom_call_target="Cholesky" | custom-call | tf_op jit(solution)/shard_map/jit(cholesky)/cholesky | solution.py:50
  611.5 4.8 select_select_fusion
  616.3 22.8 %while.1 = (s32[]{:T(128)}, f32[1024,1024]{1,0:T(8,128)}, s32[8,2]{0,1:T(2,128)S(1)}, f32[8,128,128]{2,1,0:T(8,128)S(1)}, s32[]{:T(128)}) while((s32[]{:T(128)}, f32[1024,1024]{1,0:T(8,128)}, s32[8,2]{0,1:T(2,128)S(1)}, f32[8,128,128]{2,1,0:T(8,128)S(1)}, s32[]{:T(128)}) %tuple.58), condition=%wide.while_cond, body=%wide.while_body.sunk | while | flops 2 | bytes 131181 | solution.py:51
  639.1 78.8 %custom-call.69 = f32[8,128,128]{1,2,0:T(8,128)S(1)} custom-call(f32[8,128,128]{2,1,0:T(8,128)S(1)} %get-tuple-element.13), custom_call_target="InvertDiagBlocksLowerTriangular" | custom-call | tf_op jit(solution)/shard_map/triangular_solve | solution.py:51
  (159 shorter events, 101.3 us)
Async XLA Ops:
  6.5 14.0 %copy-start = (f32[1,512,512]{2,1,0:T(8,128)S(1)}, f32[1,512,512]{2,1,0:T(8,128)}, u32[]{:S(2)}) copy-start(f32[1,512,512]{2,1,0:T(8,128)} %param.6) | copy-start | bytes 3145732
  6.5 270.1 %all-reduce.4.cloned.1.call-start = ((), (), s32[]{:S(2)}) async-start(), calls=%async_computation.1 | async-start | bytes 8388608 | tf_op jit(solution)/shard_map/psum | solution.py:48
  7.6 9.4 %collective-permute-start = (f32[128,512]{1,0:T(8,128)S(1)}, f32[128,512]{1,0:T(8,128)S(1)}, u32[]{:S(2)}, u32[]{:S(2)}) collective-permute-start(f32[128,512]{1,0:T(8,128)S(1)} %slice.283), channel_id=1, source_target_pairs={{2,0},{4,2},{6,4},{8,6},{10,8},{12,10},{14,12},{16,14},{18,16},{20... | collective-permute-start | bytes 786440 | tf_op jit(solution)/shard_map/ppermute | solution.py:15
  20.6 19.6 %copy-start.6 = (f32[384,512]{1,0:T(8,128)S(1)}, f32[384,512]{1,0:T(8,128)}, u32[]{:S(2)}) copy-start(f32[384,512]{1,0:T(8,128)} %param.5) | copy-start | bytes 2359300
  31.3 8.8 %collective-permute-start.1 = (f32[128,512]{1,0:T(8,128)S(1)}, f32[128,512]{1,0:T(8,128)S(1)}, u32[]{:S(2)}, u32[]{:S(2)}) collective-permute-start(f32[128,512]{1,0:T(8,128)S(1)} %slice.325), channel_id=1, source_target_pairs={{30,0},{0,2},{2,4},{4,6},{6,8},{8,10},{10,12},{12,14},{14,16},{16,... | collective-permute-start | bytes 786440 | tf_op jit(solution)/shard_map/ppermute | solution.py:15
  40.2 0.7 copy-start.10
  40.4 4.3 copy-start.7
  40.4 4.2 collective-permute-start.2
  57.7 8.8 %collective-permute-start.3 = (f32[128,512]{1,0:T(8,128)S(1)}, f32[128,512]{1,0:T(8,128)S(1)}, u32[]{:S(2)}, u32[]{:S(2)}) collective-permute-start(f32[128,512]{1,0:T(8,128)S(1)} %slice.329), channel_id=1, source_target_pairs={{30,0},{0,2},{2,4},{4,6},{6,8},{8,10},{10,12},{12,14},{14,16},{16,... | collective-permute-start | bytes 786440 | tf_op jit(solution)/shard_map/ppermute | solution.py:15
  67.8 4.5 copy-start.2
  67.8 4.5 collective-permute-start.4
  74.0 20.6 %copy-start.3 = (f32[384,512]{1,0:T(8,128)S(1)}, f32[384,512]{1,0:T(8,128)}, u32[]{:S(2)}) copy-start(f32[384,512]{1,0:T(8,128)} %copy-done.2) | copy-start | bytes 2359300
  85.7 8.8 %collective-permute-start.5 = (f32[128,512]{1,0:T(8,128)S(1)}, f32[128,512]{1,0:T(8,128)S(1)}, u32[]{:S(2)}, u32[]{:S(2)}) collective-permute-start(f32[128,512]{1,0:T(8,128)S(1)} %slice.333), channel_id=1, source_target_pairs={{30,0},{0,2},{2,4},{4,6},{6,8},{8,10},{10,12},{12,14},{14,16},{16,... | collective-permute-start | bytes 786440 | tf_op jit(solution)/shard_map/ppermute | solution.py:15
  96.0 4.1 collective-permute-start.6
  102.6 24.5 %copy-start.4 = (f32[384,512]{1,0:T(8,128)S(1)}, f32[384,512]{1,0:T(8,128)}, u32[]{:S(2)}) copy-start(f32[384,512]{1,0:T(8,128)} %copy-done.2) | copy-start | bytes 2359300
  117.2 8.8 %collective-permute-start.7 = (f32[128,512]{1,0:T(8,128)S(1)}, f32[128,512]{1,0:T(8,128)S(1)}, u32[]{:S(2)}, u32[]{:S(2)}) collective-permute-start(f32[128,512]{1,0:T(8,128)S(1)} %slice.337), channel_id=1, source_target_pairs={{30,0},{0,2},{2,4},{4,6},{6,8},{8,10},{10,12},{12,14},{14,16},{16,... | collective-permute-start | bytes 786440 | tf_op jit(solution)/shard_map/ppermute | solution.py:15
  127.3 4.2 copy-start.8
  127.4 4.2 collective-permute-start.8
  134.0 21.7 %copy-start.9 = (f32[384,512]{1,0:T(8,128)S(1)}, f32[384,512]{1,0:T(8,128)}, u32[]{:S(2)}) copy-start(f32[384,512]{1,0:T(8,128)} %copy-done.8) | copy-start | bytes 2359300
  146.9 8.7 %collective-permute-start.9 = (f32[128,512]{1,0:T(8,128)S(1)}, f32[128,512]{1,0:T(8,128)S(1)}, u32[]{:S(2)}, u32[]{:S(2)}) collective-permute-start(f32[128,512]{1,0:T(8,128)S(1)} %slice.341), channel_id=1, source_target_pairs={{30,0},{0,2},{2,4},{4,6},{6,8},{8,10},{10,12},{12,14},{14,16},{16,... | collective-permute-start | bytes 786440 | tf_op jit(solution)/shard_map/ppermute | solution.py:15
  171.7 219.8 %all-reduce.6.cloned.1.call-start = ((), (), s32[]{:S(2)}) async-start(), calls=%async_computation.2 | async-start | bytes 8388608 | tf_op jit(solution)/shard_map/psum | solution.py:48
  406.7 1.9 copy-start.5
  719.6 11.5 %copy-start.1 = (f32[1,512,512]{2,1,0:T(8,128)S(1)}, f32[1,512,512]{2,1,0:T(8,128)}, u32[]{:S(2)}) copy-start(f32[1,512,512]{2,1,0:T(8,128)} %param.6) | copy-start | bytes 3145732
  730.2 0.9 copy-start.11
Sparse Core Ops, SparseCore 0:
  171.8 104.8 all-reduce.3
  280.3 111.0 all-reduce.5
